TPU v7x, 32 devices: a whole 2x2x4 slice. The times are simulated.
32 devices in a mesh: groups: 1, db: 32 (over z, y, x, core).
Axes of the slice: x: 2, y: 2, z: 4, core: 2. Of those that a mesh axis runs over, the one named last changes fastest.
Arguments:
- queries: bfloat16 [512, 128, 1280], P(('groups', 'db')), may hold values from -8 to 8
- query_lengths: int32 [512], P(('groups', 'db')), may hold values from 32 to 128
- database: bfloat16 [32, 128, 1280], P(('groups', 'db')), may hold values from -8 to 8
- db_lengths: int32 [32], P(('groups', 'db')), may hold values from 32 to 128
- hit_lists: int32 [512, 16], P(('groups', 'db')), may hold values from 0 to 31, all different within a row; in each aligned block of 16 rows (0 to 15, 16 to 31, ...) at most 16 rows name the same one
Outputs:
- pair_scores: float32 [512, 16], P(('groups', 'db'))
- best: float32 [32], P(('groups', 'db'))
Inputs may be any that keep to these rules, and one draw needn't show every extreme that they name: `hit_lists`: each row names 16 different database proteins, every database protein is named by some row, and among the 16 rows of one device none is named more than 16 times.
All inputs are finite; a program needn't handle non-finite values.
Results may differ from a plain program's by a relative error of at most 0.0003.
Values may be sent and summed in bfloat16 or wider, within the bound.
A program may use at most 128 MiB of HBM per device.

v0:
```python
import functools
import math

import jax
import jax.numpy as jnp
from jax import lax
from jax.experimental import pallas as pl
from jax.experimental.pallas import tpu as pltpu
from jax.sharding import PartitionSpec as P

DEAD = -1e30
R_Z, R_X, R_Y, R_D0, R_D1, R_SC, R_SX, R_SY, R_SD0, R_SD1 = range(10)
S_UP, S_DN, S_X, S_Y, S_D0, S_D1, S_SC, S_SX, S_SY, S_SD0, S_SD1 = range(11)


def pair_sums(dots, row_limit, row_live, col_limit, col_one, scale):
    s = jnp.minimum(jnp.minimum(dots * scale, col_limit), row_limit)
    row_top = jnp.max(s, axis=1, keepdims=True)
    row_exp = jnp.exp2(s - row_top)
    row_inv = jnp.where(row_live, 1.0 / jnp.sum(row_exp, axis=1, keepdims=True), 0.0)
    col_top = jnp.max(s, axis=0, keepdims=True)
    col_exp = jnp.exp2(s - col_top)
    col_inv = col_one / jnp.sum(col_exp, axis=0, keepdims=True)
    a = row_exp * row_inv
    b = col_exp * col_inv
    w = a + b * (1.0 - a)
    return jnp.sum(w * s, axis=0, keepdims=True), jnp.sum(w, axis=0, keepdims=True)


def kernel(
    n, plane, group,
    qlen_ref, hits_ref, len_ref, q_hbm, db_hbm,
    scores_ref, best_ref,
    q, buf, lens, sim, limit, num, den, table, mine, others,
    send, recv, send_len, recv_len, best_send, best_recv, load,
):
    slabs = n // (2 * plane)
    queries, tile, features = q.shape
    scale = 1.0 / (math.sqrt(features) * math.log(2.0))
    half = tile // 2
    me = lax.axis_index("db")
    core = me % 2
    chip = (me // 2) % plane
    z = me // (2 * plane)
    x_chip = chip + 1 - 2 * (chip % 2)
    y_chip = (chip + 2) % 4
    d_chip = 3 - chip

    def at(zz, chip_, core_):
        return (zz * plane + chip_) * 2 + core_

    sib = at(z, chip, 1 - core)
    x_dev, y_dev = at(z, x_chip, core), at(z, y_chip, core)
    up, down = at(z + 1, chip, core), at(z - 1, chip, core)

    own_copy = pltpu.make_async_copy(db_hbm.at[0], buf.at[me], load.at[0])
    own_copy.start()
    len_copy = pltpu.make_async_copy(len_ref, lens.at[me], load.at[1])
    len_copy.start()
    q_copy = pltpu.make_async_copy(q_hbm, q, load.at[2])
    q_copy.start()

    barrier = pltpu.get_barrier_semaphore()

    def signal(dev):
        pl.semaphore_signal(barrier, inc=1, device_id={"db": dev})

    signal(sib)
    if plane > 1:
        signal(x_dev)
        signal(y_dev)

    @pl.when(z < slabs - 1)
    def _():
        signal(up)

    @pl.when(z > 0)
    def _():
        signal(down)

    ends = jnp.where(z > 0, 1, 0) + jnp.where(z < slabs - 1, 1, 0)
    pl.semaphore_wait(barrier, ends + (3 if plane > 1 else 1))

    def copies(index, dev, skind, rkind, zz, part=None):
        if part is None:
            piece = buf.at[index]
        else:
            piece = buf.at[index, pl.ds(part * half, half)]
        out = [pltpu.make_async_remote_copy(
            src_ref=piece, dst_ref=piece,
            send_sem=send.at[skind, zz], recv_sem=recv.at[rkind, zz],
            device_id={"db": dev})]
        if part != 1:
            out.append(pltpu.make_async_remote_copy(
                src_ref=lens.at[index], dst_ref=lens.at[index],
                send_sem=send_len.at[skind, zz], recv_sem=recv_len.at[rkind, zz],
                device_id={"db": dev}))
        return out

    def start(*args):
        for c in copies(*args):
            c.start()

    def got(index, rkind, zz, part=None):
        for c in copies(index, sib, 0, rkind, zz, part):
            c.wait_recv()

    def sent(index, skind, zz, part=None):
        for c in copies(index, sib, skind, 0, zz, part):
            c.wait_send()

    low = jnp.minimum(z, slabs - 1 - z)
    toward = jnp.where(z <= slabs - 1 - z, 1, -1)

    def order(k):
        near = jnp.where(k % 2 == 1, (k + 1) // 2, -(k // 2))
        return z + jnp.where(k <= 2 * low, near, toward * (k - low))

    def launch(k, first=False):
        zz = order(k)
        own = at(zz, chip, core)
        if not first:
            got(own, R_Z, zz)

        @pl.when((zz <= z) & (z < slabs - 1))
        def _():
            start(own, up, S_UP, R_Z, zz)

        @pl.when((zz >= z) & (z > 0))
        def _():
            start(own, down, S_DN, R_Z, zz)

        if plane > 1:
            start(own, x_dev, S_X, R_X, zz)
            start(own, y_dev, S_Y, R_Y, zz)
        start(own, sib, S_SC, R_SC, zz)

    own_copy.wait()
    len_copy.wait()
    launch(0, first=True)

    rows = lax.broadcasted_iota(jnp.int32, (tile, tile), 0)
    lanes = lax.broadcasted_iota(jnp.int32, (tile, tile), 1)
    chunks = queries // group

    def multiply(chunk, panel):
        left = q[pl.ds(chunk * group, group)].reshape(group * tile, features)
        sim[chunk % 2] = lax.dot_general(
            left, panel, (((1,), (1,)), ((), ())), preferred_element_type=jnp.float32)

    for i in range(queries):
        limit[i] = jnp.where(rows < qlen_ref[i], -DEAD, DEAD)

    def reduce(chunk, pair):
        for j in range(2):
            col_live = lanes[0:1] < lens[pair * 2 + j, 0:1]
            col_limit = jnp.where(col_live, -DEAD, DEAD)
            col_one = jnp.where(col_live, 1.0, 0.0)
            for g in range(group):
                i = chunk * group + g
                row_limit = limit[i]
                row_live = rows < qlen_ref[i]
                dots = sim[chunk % 2, g * tile:(g + 1) * tile, j * tile:(j + 1) * tile]
                top, bottom = pair_sums(dots, row_limit, row_live, col_limit, col_one, scale)
                num[j, i:i + 1] = top
                den[j, i:i + 1] = bottom

    d_lane = lax.broadcasted_iota(jnp.int32, table.shape, 1)
    table[...] = jnp.zeros_like(table)
    sim[...] = jnp.zeros_like(sim)
    num[...] = jnp.zeros_like(num)
    den[...] = jnp.ones_like(den)

    def finish(pair):
        reduce(chunks - 1, pair)
        for j in range(2):
            score = jnp.sum(num[j], axis=1, keepdims=True) * math.log(2.0)
            score = score / jnp.sum(den[j], axis=1, keepdims=True)
            table[...] = jnp.where(d_lane == pair * 2 + j, score, table[...])

    def compute(pair, before):
        panel = buf[pl.ds(pair * 2, 2)].reshape(2 * tile, features)
        multiply(0, panel)
        finish(before)
        for chunk in range(chunks - 1):
            multiply(chunk + 1, panel)
            reduce(chunk, pair)

    q_copy.wait()

    def step(t, before):
        k, j = t // plane, t % plane
        zz = order(k)
        own, other = at(zz, chip, core), at(zz, chip, 1 - core)

        @pl.when(j == 0)
        def _():
            got(other, R_SC, zz)

        @pl.when(j == (1 if plane > 1 else 0))
        def _():
            if plane > 1:
                xt, yt = at(zz, x_chip, core), at(zz, y_chip, core)
                got(xt, R_X, zz)
                start(xt, y_dev, S_D0, R_D0, zz, 0)
                start(xt, sib, S_SX, R_SX, zz)
                got(yt, R_Y, zz)
                start(yt, x_dev, S_D1, R_D1, zz, 1)
                start(yt, sib, S_SY, R_SY, zz)

            @pl.when((k + 1 < slabs) & ((k == 0) | (plane == 1)))
            def _():
                launch(k + 1)

            if plane > 1:
                got(at(zz, x_chip, 1 - core), R_SX, zz)

        spot = chip
        if plane > 1:
            @pl.when(j == 2)
            def _():
                got(at(zz, y_chip, 1 - core), R_SY, zz)

            @pl.when(j == 3)
            def _():
                @pl.when(k + 2 < slabs)
                def _():
                    launch(k + 2)

                dt, od = at(zz, d_chip, core), at(zz, d_chip, 1 - core)
                got(dt, R_D0, zz, 0)
                start(dt, sib, S_SD0, R_SD0, zz, 0)
                got(dt, R_D1, zz, 1)
                start(dt, sib, S_SD1, R_SD1, zz, 1)
                got(od, R_SD0, zz, 0)
                got(od, R_SD1, zz, 1)

            spot = jnp.where(j == 0, chip, jnp.where(j == 1, x_chip, jnp.where(j == 2, y_chip, d_chip)))
        pair = zz * plane + spot
        compute(pair, before)
        return pair

    finish(lax.fori_loop(0, slabs * plane, step, me // 2))

    scores = table[...]
    hits = hits_ref[...]
    named = jnp.zeros(scores.shape, jnp.bool_)
    picked = jnp.zeros(hits.shape, jnp.float32)
    h_lane = lax.broadcasted_iota(jnp.int32, hits.shape, 1)
    for h in range(hits.shape[1]):
        same = d_lane == hits[:, h:h + 1]
        named = named | same
        value = jnp.sum(jnp.where(same, scores, 0.0), axis=1, keepdims=True)
        picked = jnp.where(h_lane == h, value, picked)
    scores_ref[...] = picked
    local = jnp.max(jnp.where(named, scores, -10000.0), axis=0, keepdims=True)
    mine[...] = jnp.broadcast_to(local, mine.shape)

    def tell(dev, slot):
        return pltpu.make_async_remote_copy(
            src_ref=mine, dst_ref=others.at[slot], send_sem=best_send.at[dev],
            recv_sem=best_recv.at[slot], device_id={"db": dev})

    @pl.loop(1, n)
    def _(r):
        tell((me + r) % n, me).start()

    @pl.loop(0, slabs)
    def _(k):
        zz = order(k)
        own = at(zz, chip, core)

        @pl.when((zz <= z) & (z < slabs - 1))
        def _():
            sent(own, S_UP, zz)

        @pl.when((zz >= z) & (z > 0))
        def _():
            sent(own, S_DN, zz)

        sent(own, S_SC, zz)
        if plane > 1:
            sent(own, S_X, zz)
            sent(own, S_Y, zz)
            xt, yt, dt = at(zz, x_chip, core), at(zz, y_chip, core), at(zz, d_chip, core)
            sent(xt, S_D0, zz, 0)
            sent(xt, S_SX, zz)
            sent(yt, S_D1, zz, 1)
            sent(yt, S_SY, zz)
            sent(dt, S_SD0, zz, 0)
            sent(dt, S_SD1, zz, 1)

    @pl.loop(1, n)
    def _(r):
        tell((me + r) % n, (me + r) % n).wait()

    best = lax.fori_loop(
        1, n, lambda r, top: jnp.maximum(top, others[(me + r) % n]), mine[...])
    lane = lax.broadcasted_iota(jnp.int32, best.shape, 1)
    best_ref[...] = jnp.broadcast_to(
        jnp.max(jnp.where(lane == me, best, -jnp.inf), axis=1, keepdims=True), best.shape)


def body(n, plane, queries, query_lengths, database, db_lengths, hit_lists):
    count, tile, features = queries.shape
    slabs = n // (2 * plane)
    lanes = -(-n // 128) * 128
    group = math.gcd(count, 2)
    length = jnp.broadcast_to(db_lengths[:, None], (8, tile))
    vmem = pl.BlockSpec(memory_space=pltpu.VMEM)
    hbm = pl.BlockSpec(memory_space=pl.ANY)
    scores, best = pl.pallas_call(
        functools.partial(kernel, n, plane, group),
        out_shape=(
            jax.ShapeDtypeStruct(hit_lists.shape, jnp.float32),
            jax.ShapeDtypeStruct((8, lanes), jnp.float32),
        ),
        in_specs=[pl.BlockSpec(memory_space=pltpu.SMEM), vmem, hbm, hbm, hbm],
        out_specs=(vmem, vmem),
        scratch_shapes=[
            pltpu.VMEM(queries.shape, queries.dtype),
            pltpu.VMEM((n, tile, features), database.dtype),
            pltpu.VMEM((n, 8, tile), jnp.int32),
            pltpu.VMEM((2, group * tile, 2 * tile), jnp.float32),
            pltpu.VMEM((count, tile, tile), jnp.float32),
            pltpu.VMEM((2, count, tile), jnp.float32),
            pltpu.VMEM((2, count, tile), jnp.float32),
            pltpu.VMEM((count, lanes), jnp.float32),
            pltpu.VMEM((8, lanes), jnp.float32),
            pltpu.VMEM((n, 8, lanes), jnp.float32),
            pltpu.SemaphoreType.DMA((11, slabs)),
            pltpu.SemaphoreType.DMA((10, slabs)),
            pltpu.SemaphoreType.DMA((11, slabs)),
            pltpu.SemaphoreType.DMA((10, slabs)),
            pltpu.SemaphoreType.DMA((n,)),
            pltpu.SemaphoreType.DMA((n,)),
            pltpu.SemaphoreType.DMA((3,)),
        ],
        compiler_params=pltpu.CompilerParams(
            collective_id=0, has_side_effects=True, vmem_limit_bytes=60 * 1024 * 1024),
    )(query_lengths, hit_lists, length, queries, database)
    return scores, best[0, :1]


def solution(mesh):
    n = mesh.shape["db"]
    plane = 4 if mesh.shape["groups"] == 1 and n % 8 == 0 else 1
    return jax.shard_map(
        functools.partial(body, n, plane),
        mesh=mesh,
        in_specs=(
            P(("groups", "db"), None, None),
            P(("groups", "db")),
            P(("groups", "db"), None, None),
            P(("groups", "db")),
            P(("groups", "db"), None),
        ),
        out_specs=(P(("groups", "db"), None), P(("groups", "db"))),
        check_vma=False,
    )
```

profile of v0, /device:TPU:0, one launch (start us, length us, event | category | flops | bytes accessed | tf_op | source)
XLA Modules:
  0.0 81.5 jit_solution(7604745697880977017)
XLA Ops:
  1.3 0.6 broadcast_in_dim.9.len_ref
  1.9 77.1 %shard_map.68 = (f32[16,16]{1,0:T(8,128)}, f32[8,128]{1,0:T(8,128)}) custom-call(s32[16]{0:T(128)} %qlen_ref.1, s32[16,16]{1,0:T(8,128)} %hits_ref.1, s32[8,128]{1,0:T(8,128)} %broadcast_in_dim.9.len_ref, bf16[16,128,1280]{2,1,0:T(8,128)(2,1)} %q_hbm.1, bf16[1,128,1280]{2,1,0:T(8,128)(2,1)} %db_hbm.1), custom_call_target="tpu_custom_call" | custom-call | tf_op jit(solution)/shard_map/pallas_call | solution.py:312
  79.0 1.2 %slice.3 = f32[1,1]{1,0:T(1,128)} slice(f32[8,128]{1,0:T(8,128)} %get-tuple-element.5), slice={[0:1], [0:1]} | slice | bytes 8 | tf_op jit(solution)/shard_map/slice | solution.py:342
  80.2 1.3 %copy.9 = f32[16,16]{1,0:T(8,128)} copy(f32[16,16]{1,0:T(8,128)} %get-tuple-element.8) | data formatting | bytes 2048
where the time goes:
time: 81.8 us; the launch traced here: 81.5 us
  Pallas kernels  77.1 us (94%)
  local copies, waits for them, and re-layouts  3.07 us (4%)
  between operations  1.28 us (2%)
    pallas_call x1, Pallas kernels, body(): pl.pallas_call(functools.partial(kernel, n, plane, group), out_shape=(jax...  77.1 us

commit v1 on v0

--- a/solution.py
+++ b/solution.py
@@ -299,6 +299,455 @@
     lane = lax.broadcasted_iota(jnp.int32, best.shape, 1)
     best_ref[...] = jnp.broadcast_to(
         jnp.max(jnp.where(lane == me, best, -jnp.inf), axis=1, keepdims=True), best.shape)
+
+
+L_Z, L_X, L_Y, L_D, L_SC, L_SX, L_SY, L_SD = range(8)
+T_UP, T_DN, T_X, T_Y, T_DUP, T_DDN, T_DX, T_DY, T_SC, T_SX, T_SY, T_SD = range(12)
+OWN, XN, YN, DN = range(4)
+PIECE, HOP, NEAR, STEP, SLACK = 3.5, 1.5, 1.5, 2.1, 0.0
+
+
+def plan(slabs):
+    unit, first = 2 * PIECE, PIECE + HOP
+    due = {}
+    for h in range(2):
+        for j in range(1, slabs):
+            due["chain", j, h] = first + unit * (j - 1) + PIECE * h
+            due["spread", j, h] = due["chain", j, h] + 0.01
+            due["cross", j, h] = first + unit * j + PIECE * (1 + h)
+            due["diag", j, h] = first + unit * (j + 1) + PIECE * h
+        due["cross", 0, h] = first + PIECE * h - 0.01
+        due["diag", 0, h] = first + unit + 0.1
+    if slabs > 1:
+        due["late", 0, 0] = max(due["spread", slabs - 1, 1], due["cross", 1, 1]) + 0.05
+        for h in range(2):
+            due["edge", 0, h] = first + unit * slabs + PIECE
+    middle = list(range(1, slabs))
+    end = middle[1:-1] + middle[:1] + middle[-1:] if slabs > 2 else middle
+    across = [(DN, m, e) for m, e in zip(middle, end)]
+    steps = [(OWN, 0, 0), (XN, 0, 0), (YN, 0, 0)] + ([(OWN, 1, 1)] if slabs > 1 else []) + [(DN, 0, 0)]
+    for k in range(1, slabs):
+        if k + 1 < slabs:
+            steps.append((OWN, k + 1, k + 1))
+        else:
+            steps += across[:-2]
+        steps += [(XN, k, k), (YN, k, k)]
+    steps += across[-2:]
+
+    def needs(place, m, e):
+        if place == OWN:
+            return [("chain", m, 1)] if m else []
+        if place in (XN, YN):
+            return [("cross", m, 1)]
+        return [("diag", k, h) for k in (m, e) for h in range(2)] + [("edge", 0, h) for h in range(2) if e == 1]
+
+    slots, now, left = [], NEAR, sorted(due, key=lambda event: due[event])
+    for step in steps:
+        now = max([now] + [due[event] + NEAR for event in needs(*step)])
+        count = sum(due[event] <= now + SLACK for event in left)
+        slots.append(left[:count])
+        left = left[count:]
+        now += STEP
+    slots[-1] += left
+    return steps, slots
+
+
+def relay_kernel(
+    n, group,
+    qlen_ref, len_ref, hits_ref, q_hbm, db_hbm,
+    scores_ref, best_ref,
+    q, buf, lens, sim, limit, num, den, table, named, mine, others,
+    send, recv, send_len, recv_len, best_send, best_recv, load,
+):
+    plane = 4
+    slabs = n // (2 * plane)
+    steps, slots = plan(slabs)
+    queries, tile, features = q.shape
+    scale = 1.0 / (math.sqrt(features) * math.log(2.0))
+    half = tile // 2
+    me = lax.axis_index("db")
+    core = me % 2
+    chip = (me // 2) % plane
+    z = me // (2 * plane)
+    x_chip = chip + 1 - 2 * (chip % 2)
+    y_chip = (chip + 2) % 4
+    d_chip = 3 - chip
+    top = slabs - 1
+    edge = (z == 0) | (z == top)
+
+    def at(zz, chip_, core_):
+        return (zz * plane + chip_) * 2 + core_
+
+    sib = at(z, chip, 1 - core)
+    x_dev, y_dev = at(z, x_chip, core), at(z, y_chip, core)
+    up, down = at(z + 1, chip, core), at(z - 1, chip, core)
+
+    own_copy = pltpu.make_async_copy(db_hbm.at[0], buf.at[me], load.at[0])
+    own_copy.start()
+    q_copy = pltpu.make_async_copy(q_hbm, q, load.at[1])
+    q_copy.start()
+    lens[me] = jnp.full(lens.shape[1:], len_ref[0], jnp.int32)
+
+    barrier = pltpu.get_barrier_semaphore()
+
+    def signal(dev):
+        pl.semaphore_signal(barrier, inc=1, device_id={"db": dev})
+
+    signal(sib)
+    signal(x_dev)
+    signal(y_dev)
+
+    @pl.when(z < top)
+    def _():
+        signal(up)
+
+    @pl.when(z > 0)
+    def _():
+        signal(down)
+
+    pl.semaphore_wait(barrier, jnp.where(z > 0, 1, 0) + jnp.where(z < top, 1, 0) + 3)
+
+    def copies(index, dev, skind, rkind, zz, h):
+        piece = buf.at[index, pl.ds(h * half, half)]
+        out = [pltpu.make_async_remote_copy(
+            src_ref=piece, dst_ref=piece,
+            send_sem=send.at[skind, zz, h], recv_sem=recv.at[rkind, zz, h],
+            device_id={"db": dev})]
+        if h == 0:
+            out.append(pltpu.make_async_remote_copy(
+                src_ref=lens.at[index], dst_ref=lens.at[index],
+                send_sem=send_len.at[skind, zz], recv_sem=recv_len.at[rkind, zz],
+                device_id={"db": dev}))
+        return out
+
+    def start(*args):
+        for c in copies(*args):
+            c.start()
+
+    def got(index, rkind, zz, h):
+        for c in copies(index, sib, 0, rkind, zz, h):
+            c.wait_recv()
+
+    def sent(index, skind, zz, h):
+        for c in copies(index, sib, skind, 0, zz, h):
+            c.wait_send()
+
+    low = jnp.minimum(z, top - z)
+    toward = jnp.where(z <= top - z, 1, -1)
+
+    def order(k):
+        near = jnp.where(k % 2 == 1, (k + 1) // 2, -(k // 2))
+        return z + jnp.where(k <= 2 * low, near, toward * (k - low))
+
+    def goes_up(zz):
+        return (zz <= z) & (z < top)
+
+    def goes_down(zz):
+        return (zz >= z) & (z > 0)
+
+    def d_goes_up(zz):
+        return goes_up(zz) & ((z + 1 != top) | (zz != top - 1))
+
+    def d_goes_down(zz):
+        return goes_down(zz) & ((z != 1) | (zz != 1))
+
+    def launch(zz, h):
+        own = at(zz, chip, core)
+
+        @pl.when(goes_up(zz))
+        def _():
+            start(own, up, T_UP, L_Z, zz, h)
+
+        @pl.when(goes_down(zz))
+        def _():
+            start(own, down, T_DN, L_Z, zz, h)
+
+        start(own, sib, T_SC, L_SC, zz, h)
+
+    def both_ways(j, action):
+        @pl.when(z + j <= top)
+        def _():
+            action(z + j)
+
+        @pl.when(z - j >= 0)
+        def _():
+            action(z - j)
+
+    def chain(j, h):
+        def arrived(zz):
+            got(at(zz, chip, core), L_Z, zz, h)
+            launch(zz, h)
+        both_ways(j, arrived)
+
+    def spread(k, h):
+        zz = order(k)
+        own = at(zz, chip, core)
+        start(own, x_dev, T_X, L_X, zz, h)
+        start(own, y_dev, T_Y, L_Y, zz, 1 - h if k == 0 else h)
+
+    def turn(zz, h):
+        if h == 0:
+            start(at(zz, x_chip, core), y_dev, T_DY, L_D, zz, 0)
+        else:
+            start(at(zz, y_chip, core), x_dev, T_DX, L_D, zz, 1)
+
+    def cross(k, h):
+        zz = order(k)
+        xt, yt = at(zz, x_chip, core), at(zz, y_chip, core)
+        g = 1 - h if k == 0 else h
+        got(xt, L_X, zz, h)
+        if k == 0 and h == 0:
+            turn(zz, 0)
+        start(xt, sib, T_SX, L_SX, zz, h)
+        got(yt, L_Y, zz, g)
+        if k == 0 and h == 0:
+            turn(zz, 1)
+        start(yt, sib, T_SY, L_SY, zz, g)
+
+    def d_arrived(zz, h):
+        dt = at(zz, d_chip, core)
+        got(dt, L_D, zz, h)
+
+        @pl.when(d_goes_up(zz))
+        def _():
+            start(dt, up, T_DUP, L_D, zz, h)
+
+        @pl.when(d_goes_down(zz))
+        def _():
+            start(dt, down, T_DDN, L_D, zz, h)
+
+        start(dt, sib, T_SD, L_SD, zz, h)
+
+    def diag(j, h):
+        if j == 0:
+            d_arrived(z, h)
+        elif j == 1:
+            @pl.when(~edge)
+            def _():
+                both_ways(1, lambda zz: d_arrived(zz, h))
+        else:
+            both_ways(j, lambda zz: d_arrived(zz, h))
+
+    def late(_, __):
+        @pl.when(edge)
+        def _():
+            for h in range(2):
+                turn(order(1), h)
+
+    def edge_arrived(_, h):
+        @pl.when(edge)
+        def _():
+            d_arrived(order(1), h)
+
+    actions = {"chain": chain, "spread": spread, "cross": cross, "diag": diag, "late": late, "edge": edge_arrived}
+
+    own_copy.wait()
+    for h in range(2):
+        launch(z, h)
+        spread(0, h)
+
+    rows = lax.broadcasted_iota(jnp.int32, (tile, tile), 0)
+    lanes = lax.broadcasted_iota(jnp.int32, (tile, tile), 1)
+    chunks = queries // group
+
+    def multiply(chunk, panel):
+        left = q[pl.ds(chunk * group, group)].reshape(group * tile, features)
+        sim[chunk % 2] = lax.dot_general(
+            left, panel, (((1,), (1,)), ((), ())), preferred_element_type=jnp.float32)
+
+    for i in range(queries):
+        limit[i] = jnp.where(rows < qlen_ref[i], -DEAD, DEAD)
+
+    def reduce(chunk, pair):
+        for j in range(2):
+            col_live = lanes[0:1] < lens[pair * 2 + j]
+            col_limit = jnp.where(col_live, -DEAD, DEAD)
+            col_one = jnp.where(col_live, 1.0, 0.0)
+            for g in range(group):
+                i = chunk * group + g
+                row_limit = limit[i]
+                row_live = rows < qlen_ref[i]
+                dots = sim[chunk % 2, g * tile:(g + 1) * tile, j * tile:(j + 1) * tile]
+                above, below = pair_sums(dots, row_limit, row_live, col_limit, col_one, scale)
+                num[j, i:i + 1] = above
+                den[j, i:i + 1] = below
+
+    d_lane = lax.broadcasted_iota(jnp.int32, table.shape, 1)
+    table[...] = jnp.zeros_like(table)
+    sim[...] = jnp.zeros_like(sim)
+    num[...] = jnp.zeros_like(num)
+    den[...] = jnp.ones_like(den)
+    hits = hits_ref[...]
+    same = [d_lane == hits[:, h:h + 1] for h in range(hits.shape[1])]
+    named[...] = jnp.where(functools.reduce(jnp.logical_or, same), 1.0, 0.0)
+
+    def finish(pair):
+        reduce(chunks - 1, pair)
+        for j in range(2):
+            d = pair * 2 + j
+            score = jnp.sum(num[j], axis=1, keepdims=True) * math.log(2.0)
+            score = score / jnp.sum(den[j], axis=1, keepdims=True)
+            here = d_lane == d
+            table[...] = jnp.where(here, score, table[...])
+            counted = jnp.where(here & (named[...] > 0.0), score, -10000.0)
+            local = jnp.max(jnp.max(counted, axis=0, keepdims=True), axis=1, keepdims=True)
+            mine[d] = jnp.broadcast_to(local, mine.shape[1:])
+
+    def compute(pair, before):
+        panel = buf[pl.ds(pair * 2, 2)].reshape(2 * tile, features)
+        multiply(0, panel)
+        finish(before)
+        for chunk in range(chunks - 1):
+            multiply(chunk + 1, panel)
+            reduce(chunk, pair)
+
+    def tell(d, slot):
+        return pltpu.make_async_remote_copy(
+            src_ref=mine.at[d], dst_ref=others.at[slot], send_sem=best_send.at[d],
+            recv_sem=best_recv.at[slot], device_id={"db": d})
+
+    def tell_pair(pair):
+        for j in range(2):
+            d = pair * 2 + j
+
+            @pl.when(d != me)
+            def _():
+                tell(d, me).start()
+
+    def pick(t, values):
+        out = jnp.int32(values[0])
+        for i in range(1, len(values)):
+            if values[i] != values[i - 1]:
+                out = jnp.where(t >= i, values[i], out)
+        return out
+
+    q_copy.wait()
+
+    def step(t, carry):
+        before, done = carry
+        for number, events in enumerate(slots):
+            if events:
+                @pl.when(t == number)
+                def _(events=events):
+                    for kind, index, h in events:
+                        actions[kind](index, h)
+
+        @pl.when(t >= 2)
+        def _():
+            tell_pair(done)
+
+        place = pick(t, [p for p, _, _ in steps])
+        k = jnp.where(edge, pick(t, [e for _, _, e in steps]), pick(t, [m for _, m, _ in steps]))
+        zz = order(k)
+        for number, (kind, spot) in enumerate(((L_SC, chip), (L_SX, x_chip), (L_SY, y_chip), (L_SD, d_chip))):
+            @pl.when(place == number)
+            def _(kind=kind, spot=spot):
+                for h in range(2):
+                    got(at(zz, spot, 1 - core), kind, zz, h)
+
+        spot = jnp.where(place == OWN, chip, jnp.where(place == XN, x_chip, jnp.where(place == YN, y_chip, d_chip)))
+        pair = zz * plane + spot
+        compute(pair, before)
+        return pair, before
+
+    last, done = lax.fori_loop(0, len(steps), step, (me // 2, me // 2))
+    tell_pair(done)
+    finish(last)
+    tell_pair(last)
+
+    scores = table[...]
+    picked = jnp.zeros(hits.shape, jnp.float32)
+    h_lane = lax.broadcasted_iota(jnp.int32, hits.shape, 1)
+    for h in range(hits.shape[1]):
+        value = jnp.sum(jnp.where(d_lane == hits[:, h:h + 1], scores, 0.0), axis=1, keepdims=True)
+        picked = jnp.where(h_lane == h, value, picked)
+    scores_ref[...] = picked
+
+    @pl.loop(0, slabs)
+    def _(zz):
+        own, dt = at(zz, chip, core), at(zz, d_chip, core)
+        xt, yt = at(zz, x_chip, core), at(zz, y_chip, core)
+        near_edge = edge & (zz == order(1)) if slabs > 1 else jnp.bool_(False)
+        for h in range(2):
+            @pl.when(goes_up(zz))
+            def _():
+                sent(own, T_UP, zz, h)
+
+            @pl.when(goes_down(zz))
+            def _():
+                sent(own, T_DN, zz, h)
+
+            @pl.when(d_goes_up(zz))
+            def _():
+                sent(dt, T_DUP, zz, h)
+
+            @pl.when(d_goes_down(zz))
+            def _():
+                sent(dt, T_DDN, zz, h)
+
+            @pl.when((zz == z) | near_edge)
+            def _():
+                if h == 0:
+                    sent(xt, T_DY, zz, 0)
+                else:
+                    sent(yt, T_DX, zz, 1)
+
+            sent(own, T_X, zz, h)
+            sent(own, T_Y, zz, h)
+            sent(own, T_SC, zz, h)
+            sent(xt, T_SX, zz, h)
+            sent(yt, T_SY, zz, h)
+            sent(dt, T_SD, zz, h)
+
+    others[me] = mine[me]
+
+    @pl.loop(1, n)
+    def _(r):
+        tell((me + r) % n, (me + r) % n).wait()
+
+    best_ref[...] = jnp.broadcast_to(jnp.max(others[...], axis=0), best_ref.shape)
+
+
+def relay_body(n, queries, query_lengths, database, db_lengths, hit_lists):
+    count, tile, features = queries.shape
+    slabs = n // 8
+    lanes = -(-n // 128) * 128
+    group = math.gcd(count, 2)
+    vmem = pl.BlockSpec(memory_space=pltpu.VMEM)
+    smem = pl.BlockSpec(memory_space=pltpu.SMEM)
+    hbm = pl.BlockSpec(memory_space=pl.ANY)
+    scores, best = pl.pallas_call(
+        functools.partial(relay_kernel, n, group),
+        out_shape=(
+            jax.ShapeDtypeStruct(hit_lists.shape, jnp.float32),
+            jax.ShapeDtypeStruct((8, tile), jnp.float32),
+        ),
+        in_specs=[smem, smem, vmem, hbm, hbm],
+        out_specs=(vmem, vmem),
+        scratch_shapes=[
+            pltpu.VMEM(queries.shape, queries.dtype),
+            pltpu.VMEM((n, tile, features), database.dtype),
+            pltpu.VMEM((n, 1, tile), jnp.int32),
+            pltpu.VMEM((2, group * tile, 2 * tile), jnp.float32),
+            pltpu.VMEM((count, tile, tile), jnp.float32),
+            pltpu.VMEM((2, count, tile), jnp.float32),
+            pltpu.VMEM((2, count, tile), jnp.float32),
+            pltpu.VMEM((count, lanes), jnp.float32),
+            pltpu.VMEM((count, lanes), jnp.float32),
+            pltpu.VMEM((n, 1, tile), jnp.float32),
+            pltpu.VMEM((n, 1, tile), jnp.float32),
+            pltpu.SemaphoreType.DMA((12, slabs, 2)),
+            pltpu.SemaphoreType.DMA((8, slabs, 2)),
+            pltpu.SemaphoreType.DMA((12, slabs)),
+            pltpu.SemaphoreType.DMA((8, slabs)),
+            pltpu.SemaphoreType.DMA((n,)),
+            pltpu.SemaphoreType.DMA((n,)),
+            pltpu.SemaphoreType.DMA((2,)),
+        ],
+        compiler_params=pltpu.CompilerParams(
+            collective_id=0, has_side_effects=True, vmem_limit_bytes=60 * 1024 * 1024),
+    )(query_lengths, db_lengths, hit_lists, queries, database)
+    return scores, best[0, :1]
 
 
 def body(n, plane, queries, query_lengths, database, db_lengths, hit_lists):
@@ -345,8 +794,9 @@
 def solution(mesh):
     n = mesh.shape["db"]
     plane = 4 if mesh.shape["groups"] == 1 and n % 8 == 0 else 1
+    work = functools.partial(relay_body, n) if plane == 4 else functools.partial(body, n, plane)
     return jax.shard_map(
-        functools.partial(body, n, plane),
+        work,
         mesh=mesh,
         in_specs=(
             P(("groups", "db"), None, None),

time: 81.8 us -> 66.9 us (0.82)
  Pallas kernels: 77.1 us -> 62.8 us
    pallas_call x1, Pallas kernels: 77.1 us -> 62.8 us  [relay_body(): pl.pallas_call(functools.partial(relay_kernel, n, group), out_shape=(jax....]
where the time goes in v1:
time: 66.9 us; the launch traced here: 66.5 us
  Pallas kernels  62.8 us (94%)
  local copies, waits for them, and re-layouts  2.48 us (4%)
  between operations  1.29 us (2%)
    pallas_call x1, Pallas kernels, relay_body(): pl.pallas_call(functools.partial(relay_kernel, n, group), out_shape=(jax....  62.8 us

profile of v1, /device:TPU:0, one launch (start us, length us, event | category | flops | bytes accessed | tf_op | source)
XLA Modules:
  0.0 66.5 jit_solution(8181020582376123556)
XLA Ops:
  1.3 62.8 %shard_map.68 = (f32[16,16]{1,0:T(8,128)}, f32[8,128]{1,0:T(8,128)}) custom-call(s32[16]{0:T(128)} %qlen_ref.1, s32[1]{0:T(128)S(6)} %copy.8.len_ref, s32[16,16]{1,0:T(8,128)} %hits_ref.1, bf16[16,128,1280]{2,1,0:T(8,128)(2,1)} %q_hbm.1, bf16[1,128,1280]{2,1,0:T(8,128)(2,1)} %db_hbm.1), custom_call_target="tpu_custom_call" | custom-call | tf_op jit(solution)/shard_map/pallas_call | solution.py:719
  64.1 1.2 %slice.3 = f32[1,1]{1,0:T(1,128)} slice(f32[8,128]{1,0:T(8,128)} %get-tuple-element.5), slice={[0:1], [0:1]} | slice | bytes 8 | tf_op jit(solution)/shard_map/slice | solution.py:750
  65.2 1.3 %copy.9 = f32[16,16]{1,0:T(8,128)} copy(f32[16,16]{1,0:T(8,128)} %get-tuple-element.8) | data formatting | bytes 2048

commit v2 on v1

--- a/solution.py
+++ b/solution.py
@@ -304,7 +304,23 @@
 L_Z, L_X, L_Y, L_D, L_SC, L_SX, L_SY, L_SD = range(8)
 T_UP, T_DN, T_X, T_Y, T_DUP, T_DDN, T_DX, T_DY, T_SC, T_SX, T_SY, T_SD = range(12)
 OWN, XN, YN, DN = range(4)
-PIECE, HOP, NEAR, STEP, SLACK = 3.5, 1.5, 1.5, 2.1, 0.0
+LEAST = 32
+PIECE, HOP, NEAR, STEP, SLACK = 3.5, 1.5, 1.5, 2.1, 2.2
+
+
+def capped_sums(dots, row_limit, row_cap, col_limit, col_one, scale):
+    s = jnp.minimum(dots * scale, col_limit)
+    s = jnp.concatenate([s[:LEAST], jnp.minimum(s[LEAST:], row_limit[LEAST:])], axis=0)
+    row_exp = jnp.exp2(s - jnp.max(s, axis=1, keepdims=True))
+    row_inv = jnp.broadcast_to(1.0 / jnp.sum(row_exp, axis=1, keepdims=True), dots.shape)
+    row_inv = jnp.concatenate([row_inv[:LEAST], jnp.minimum(row_inv[LEAST:], row_cap[LEAST:])], axis=0)
+    col_top = jnp.max(s, axis=0, keepdims=True)
+    col_exp = jnp.exp2(s - col_top)
+    col_inv = col_one / jnp.sum(col_exp, axis=0, keepdims=True)
+    a = row_exp * row_inv
+    b = col_exp * col_inv
+    w = a + b * (1.0 - a)
+    return jnp.sum(w * s, axis=0, keepdims=True), jnp.sum(w, axis=0, keepdims=True)
 
 
 def plan(slabs):
@@ -356,7 +372,7 @@
     n, group,
     qlen_ref, len_ref, hits_ref, q_hbm, db_hbm,
     scores_ref, best_ref,
-    q, buf, lens, sim, limit, num, den, table, named, mine, others,
+    q, buf, lens, sim, limit, cap, num, den, table, named, mine, others,
     send, recv, send_len, recv_len, best_send, best_recv, load,
 ):
     plane = 4
@@ -557,6 +573,7 @@
 
     for i in range(queries):
         limit[i] = jnp.where(rows < qlen_ref[i], -DEAD, DEAD)
+        cap[i] = jnp.where(rows < qlen_ref[i], 1.0, 0.0)
 
     def reduce(chunk, pair):
         for j in range(2):
@@ -565,10 +582,8 @@
             col_one = jnp.where(col_live, 1.0, 0.0)
             for g in range(group):
                 i = chunk * group + g
-                row_limit = limit[i]
-                row_live = rows < qlen_ref[i]
                 dots = sim[chunk % 2, g * tile:(g + 1) * tile, j * tile:(j + 1) * tile]
-                above, below = pair_sums(dots, row_limit, row_live, col_limit, col_one, scale)
+                above, below = capped_sums(dots, limit[i], cap[i], col_limit, col_one, scale)
                 num[j, i:i + 1] = above
                 den[j, i:i + 1] = below
 
@@ -729,6 +744,7 @@
             pltpu.VMEM((n, tile, features), database.dtype),
             pltpu.VMEM((n, 1, tile), jnp.int32),
             pltpu.VMEM((2, group * tile, 2 * tile), jnp.float32),
+            pltpu.VMEM((count, tile, tile), jnp.float32),
             pltpu.VMEM((count, tile, tile), jnp.float32),
             pltpu.VMEM((2, count, tile), jnp.float32),
             pltpu.VMEM((2, count, tile), jnp.float32),

time: 66.9 us -> 63.8 us (0.954)
  Pallas kernels: 62.8 us -> 59.7 us
    pallas_call x1, Pallas kernels: 62.8 us -> 59.7 us  [relay_body(): pl.pallas_call(functools.partial(relay_kernel, n, group), out_shape=(jax....]
where the time goes in v2:
time: 63.8 us; the launch traced here: 63.5 us
  Pallas kernels  59.7 us (94%)
  local copies, waits for them, and re-layouts  2.48 us (4%)
  between operations  1.29 us (2%)
    pallas_call x1, Pallas kernels, relay_body(): pl.pallas_call(functools.partial(relay_kernel, n, group), out_shape=(jax....  59.7 us
    unnamed x1, local copies, waits for them, and re-layouts  1.29 us

profile of v2, /device:TPU:0, one launch (start us, length us, event | category | flops | bytes accessed | tf_op | source)
XLA Modules:
  0.0 63.5 jit_solution(5019563469753309633)
XLA Ops:
  1.3 59.7 %shard_map.68 = (f32[16,16]{1,0:T(8,128)}, f32[8,128]{1,0:T(8,128)}) custom-call(s32[16]{0:T(128)} %qlen_ref.1, s32[1]{0:T(128)S(6)} %copy.8.len_ref, s32[16,16]{1,0:T(8,128)} %hits_ref.1, bf16[16,128,1280]{2,1,0:T(8,128)(2,1)} %q_hbm.1, bf16[1,128,1280]{2,1,0:T(8,128)(2,1)} %db_hbm.1), custom_call_target="tpu_custom_call" | custom-call | tf_op jit(solution)/shard_map/pallas_call | solution.py:734
  61.0 1.2 %slice.3 = f32[1,1]{1,0:T(1,128)} slice(f32[8,128]{1,0:T(8,128)} %get-tuple-element.5), slice={[0:1], [0:1]} | slice | bytes 8 | tf_op jit(solution)/shard_map/slice | solution.py:766
  62.2 1.3 %copy.9 = f32[16,16]{1,0:T(8,128)} copy(f32[16,16]{1,0:T(8,128)} %get-tuple-element.8) | data formatting | bytes 2048
